TPU v7x, 256 devices: a whole 4x4x8 slice. The times are simulated.
256 devices in a mesh: dp: 32 (over z, y), grp: 8 (over x, core).
Axes of the slice: x: 4, y: 4, z: 8, core: 2. Of those that a mesh axis runs over, the one named last changes fastest.
Arguments:
- tokens: bfloat16 [1024, 256, 1024], P(('dp', 'grp')), may hold values from -0.1875 to 0.1875
- patches: bfloat16 [1024, 256, 1024], P(('dp', 'grp')), may hold values from -0.1875 to 0.1875
- lengths: int32 [1024], P(('dp', 'grp')), may hold values from 16 to 256, as said below
- img_pooled: bfloat16 [1024, 1024], P(('dp', 'grp')), may hold values from -1 to 1
- txt_pooled: bfloat16 [1024, 1024], P(('dp', 'grp')), may hold values from -1 to 1
Outputs:
- grad_tokens: bfloat16 [1024, 256, 1024], P(('dp', 'grp'))
- grad_patches: bfloat16 [1024, 256, 1024], P(('dp', 'grp'))
- grad_img: bfloat16 [1024, 1024], P(('dp', 'grp'))
- grad_txt: bfloat16 [1024, 1024], P(('dp', 'grp'))
- loss_mean: float32 [], replicated
Inputs may be any that keep to these rules, and one draw needn't show every extreme that they name: `lengths`: among the pairs of one index of dp (8 devices along grp), exactly 8 captions have more than 128 tokens; no device holds more than two of them and some device holds two; some caption has exactly 256 tokens and some exactly 128.
All inputs are finite; a program needn't handle non-finite values.
Results may differ from a plain program's by a relative error of at most 0.013.
Values may be sent and summed in bfloat16 or wider, within the bound.
A program may use at most 128 MiB of HBM per device.

v0:
```python
import jax
import jax.numpy as jnp
from jax import lax
from jax.sharding import Mesh
from jax.sharding import PartitionSpec as P

DP_GRP = ("dp_0", "dp_1", "grp_0", "grp_1")
RANGE_EPS = 1e-06
NORM_EPS = 1e-06
GLOBAL_SCALE = 100.0
FINE_SCALE = 50.0
MASK_FILL = -1000000000.0


def side_by_side(arrays, axis, dim, along):
    ends, at = ([], 0)
    for a in arrays[:-1]:
        at += a.shape[along]
        ends.append(at)
    both = jnp.concatenate(arrays, axis=along)
    return tuple(jnp.split(lax.all_gather(both, axis, axis=dim, tiled=True), ends, axis=along))


def gather_turned(arrays, axis, dims):
    turned = [jnp.moveaxis(a, dim, 0) for a, dim in zip(arrays, dims)]
    both = jnp.concatenate([t.reshape(len(t), -1) for t in turned], axis=1)
    filled, at, gathered = (lax.all_gather(both, axis, axis=0, tiled=True), 0, [])
    for t, dim in zip(turned, dims):
        section = filled[:, at : at + t[0].size].reshape(-1, *t.shape[1:])
        gathered.append(jnp.moveaxis(section, 0, dim))
        at += t[0].size
    return tuple(gathered)


def over_axes(array, axes):
    for axis in axes:
        array = lax.psum(array, axis)
    return array


def pair_terms(tok_rows, patch_rows, length):
    patch_count = patch_rows.shape[0]
    slot_count = tok_rows.shape[0]
    similar = jnp.dot(tok_rows, patch_rows.T, preferred_element_type=jnp.float32)
    lowest = jnp.min(similar, 1, keepdims=True)
    highest = jnp.max(similar, 1, keepdims=True)
    scaled = (similar - lowest) / (highest - lowest + RANGE_EPS)
    weights = jnp.maximum(scaled - 1.0 / patch_count, 0.0)
    weights = weights / jnp.sum(weights, 1, keepdims=True)
    grouped = jnp.dot(weights.astype(jnp.bfloat16), patch_rows, preferred_element_type=jnp.float32)
    group_unit = grouped * lax.rsqrt(jnp.sum(grouped * grouped, 1, keepdims=True) + NORM_EPS)
    token_float = tok_rows.astype(jnp.float32)
    token_unit = token_float * lax.rsqrt(
        jnp.sum(token_float * token_float, 1, keepdims=True) + NORM_EPS
    )
    logits = FINE_SCALE * jnp.dot(
        group_unit.astype(jnp.bfloat16),
        token_unit.astype(jnp.bfloat16).T,
        preferred_element_type=jnp.float32,
    )
    position = jnp.arange(slot_count, dtype=jnp.int32)
    valid = position < length
    both_valid = jnp.logical_and(valid[:, None], valid[None, :])
    masked = jnp.where(both_valid, logits, MASK_FILL)
    row_lse = jax.nn.logsumexp(masked, 1)
    col_lse = jax.nn.logsumexp(masked, 0)
    per_token = jnp.where(valid, row_lse + col_lse - 2.0 * jnp.diagonal(logits), 0.0)
    return jnp.sum(per_token) / (2.0 * length.astype(jnp.float32))


def pair_grads(tok_rows, patch_rows, length):

    def closure(first_arg, second_arg):
        return pair_terms(first_arg, second_arg, length)

    value, pullback = jax.vjp(closure, tok_rows, patch_rows)
    grad_tok, grad_patch = pullback(jnp.ones((), jnp.float32))
    return (value, grad_tok, grad_patch)


def fine_block(tok_rows, patch_rows, length_rows):
    return jax.vmap(pair_grads)(tok_rows, patch_rows, length_rows)


def unit_rows(pooled):
    values = pooled.astype(jnp.float32)
    inverse = lax.rsqrt(jnp.sum(values * values, -1, keepdims=True) + NORM_EPS)
    return (values * inverse, inverse)


def body(tokens, patches, lengths, img_pooled, txt_pooled):
    img_unit, img_inverse = unit_rows(img_pooled)
    txt_unit, txt_inverse = unit_rows(txt_pooled)
    img_half = img_unit.astype(jnp.bfloat16)
    txt_half = txt_unit.astype(jnp.bfloat16)
    all_img, all_txt = side_by_side((img_half, txt_half), DP_GRP, 0, 1)
    local_pairs = img_half.shape[0]
    pair_total = all_img.shape[0]
    offset = lax.axis_index(DP_GRP) * local_pairs
    own_mask = (
        jnp.arange(pair_total, dtype=jnp.int32)[None, :]
        == offset + jnp.arange(local_pairs, dtype=jnp.int32)[:, None]
    ).astype(jnp.float32)
    row_logits = GLOBAL_SCALE * jnp.dot(img_half, all_txt.T, preferred_element_type=jnp.float32)
    col_logits = GLOBAL_SCALE * jnp.dot(txt_half, all_img.T, preferred_element_type=jnp.float32)
    row_lse = jax.nn.logsumexp(row_logits, 1)
    col_lse = jax.nn.logsumexp(col_logits, 1)
    matches = GLOBAL_SCALE * jnp.sum(
        img_half.astype(jnp.float32) * txt_half.astype(jnp.float32), -1
    )
    global_part = 0.5 * jnp.sum(row_lse + col_lse - 2.0 * matches)
    row_own = (0.5 * jnp.exp(row_logits - row_lse[:, None]) - 0.5 * own_mask).astype(jnp.bfloat16)
    col_own = (0.5 * jnp.exp(col_logits - col_lse[:, None]) - 0.5 * own_mask).astype(jnp.bfloat16)
    img_local = jnp.dot(row_own, all_txt, preferred_element_type=jnp.float32)
    txt_local = jnp.dot(col_own, all_img, preferred_element_type=jnp.float32)
    lse_rows, lse_cols = gather_turned((row_lse, col_lse), DP_GRP, (0, 0))
    col_rows = (0.5 * jnp.exp(row_logits - lse_cols[None, :]) - 0.5 * own_mask).astype(jnp.bfloat16)
    row_cols = (0.5 * jnp.exp(col_logits - lse_rows[None, :]) - 0.5 * own_mask).astype(jnp.bfloat16)
    img_dir = GLOBAL_SCALE * (
        img_local + jnp.dot(col_rows, all_txt, preferred_element_type=jnp.float32)
    )
    txt_dir = GLOBAL_SCALE * (
        txt_local + jnp.dot(row_cols, all_img, preferred_element_type=jnp.float32)
    )
    grad_img = (
        (img_dir - img_unit * jnp.sum(img_unit * img_dir, -1, keepdims=True)) * img_inverse
    ).astype(jnp.bfloat16)
    grad_txt = (
        (txt_dir - txt_unit * jnp.sum(txt_unit * txt_dir, -1, keepdims=True)) * txt_inverse
    ).astype(jnp.bfloat16)
    values, grad_tokens, grad_patches = fine_block(tokens, patches, lengths)
    summed_loss = over_axes(global_part + jnp.sum(values), DP_GRP)
    loss_mean = summed_loss / pair_total
    return (grad_tokens, grad_patches, grad_img, grad_txt, loss_mean)


def solution(mesh):
    finer = Mesh(mesh.devices.reshape(8, 4, 4, 2), ("dp_0", "dp_1", "grp_0", "grp_1"))
    placed = (
        P(DP_GRP, None, None),
        P(DP_GRP, None, None),
        P(DP_GRP),
        P(DP_GRP, None),
        P(DP_GRP, None),
    )
    return jax.shard_map(
        body,
        mesh=finer,
        in_specs=placed,
        out_specs=(
            P(DP_GRP, None, None),
            P(DP_GRP, None, None),
            P(DP_GRP, None),
            P(DP_GRP, None),
            P(),
        ),
        check_vma=False,
    )
```

profile of v0, /device:TPU:1, one launch (start us, length us, event | category | flops | bytes accessed | tf_op | source)
XLA Modules:
  0.0 264.1 jit_solution(3292715968489793611)
XLA Ops:
  7.2 0.0 copy-start
  7.2 0.0 copy-start.14
  7.2 0.0 all-gather.4.cloned.1.call-start
  7.2 1.0 fusion.82
  8.2 0.8 fusion.77
  9.0 0.9 multiply_reduce_fusion.2
  9.9 0.6 maximum_bitcast_fusion
  10.5 0.0 all-gather.4.cloned.1.call-update
  10.6 2.1 fusion.2
  12.6 0.0 copy-done
  12.7 2.4 fusion.133
  15.0 0.0 copy-start.6
  15.0 0.1 iota_compare_fusion.1
  15.1 0.2 maximum_reduce_fusion
  15.3 0.0 copy-start.4
  15.3 0.9 multiply_reduce_fusion
  16.3 1.9 copy-done.1
  18.2 2.0 fusion.58
  20.2 16.5 %copy.71 = f32[4,256,256]{0,2,1:T(8,128)} copy(f32[4,256,256]{1,2,0:T(8,128)S(1)} %get-tuple-element.46) | data formatting | bytes 2097152 | tf_op jit(solution)/shard_map/vmap(jvp())/mul | solution.py:56
  36.7 2.3 gather_fusion
  39.1 0.1 copy.77
  39.1 0.5 fusion.55
  39.7 0.3 fusion.56
  40.0 0.2 fusion.110
  40.2 1.4 and_select_fusion
  41.7 17.4 %copy.65 = f32[4,256,256]{0,2,1:T(8,128)} copy(f32[4,256,256]{1,2,0:T(8,128)} %and_select_fusion) | data formatting | bytes 2097152 | tf_op jit(solution)/shard_map/vmap(transpose(jvp(jit(_where))))/select_n | solution.py:64
  59.1 0.1 copy.66
  59.2 26.1 %scatter_fusion = f32[4,256,256]{0,2,1:T(8,128)} fusion(f32[4,256,256]{0,2,1:T(8,128)} %copy.65, s32[256]{0:T(256)S(1)} %bitcast.34, f32[256,4]{1,0:T(8,128)S(1)} %copy.66), kind=kCustom, calls=%fused_computation.1 | custom fusion | flops 1024 | bytes 14336 | tf_op jit(solution)/shard_map/vmap(transpose(jvp(jit(diagonal))))/cond/branch_0_fun/scatter-add | solution.py:67
  85.3 19.1 %copy.67 = f32[4,256,256]{1,2,0:T(8,128)S(1)} copy(f32[4,256,256]{0,2,1:T(8,128)} %scatter_fusion) | data formatting | bytes 2097152 | tf_op jit(solution)/shard_map/vmap(transpose(jvp(jit(diagonal))))/cond/branch_0_fun/scatter-add | solution.py:67
  104.4 0.0 copy-start.7
  104.4 4.3 %fusion = (f32[4,256]{1,0:T(4,128)S(1)}, bf16[4,256,1024]{2,1,0:T(8,128)(2,1)S(1)}) fusion(f32[4,256,1024]{2,1,0:T(8,128)} %copy-done.1, bf16[4,256,1024]{2,1,0:T(8,128)(2,1)} %param.5, f32[4,256]{1,0:T(4,128)S(1)} %get-tuple-element.61, f32[4,256,256]{1,2,0:T(8,128)S(1)} %copy.67), kind=kOutput, calls=%fused_computation.11 | convolution fusion | flops 544472064 | bytes 9445376 | tf_op jit(solution)/shard_map/vmap(transpose(jvp()))/dot_general | solution.py:56
  108.7 0.0 copy-start.9
  108.7 0.3 copy-done.7
  109.0 2.2 fusion.52
  111.2 0.6 divide_reduce_fusion
  111.8 4.3 %fusion.4 = (f32[4,256]{1,0:T(4,128)S(1)}, bf16[4,256,1024]{2,1,0:T(8,128)(2,1)S(1)}) fusion(bf16[4,256,1024]{2,1,0:T(8,128)(2,1)} %param.5, f32[4,256,1024]{2,1,0:T(8,128)} %copy-done.1, f32[4,256]{1,0:T(4,128)S(1)} %get-tuple-element.62, f32[4,256,256]{1,2,0:T(8,128)S(1)} %copy.67), kind=kOutput, calls=%fused_computation.15 | convolution fusion | flops 544472064 | bytes 9445376 | tf_op jit(solution)/shard_map/vmap(transpose(jvp()))/dot_general | solution.py:56
  116.1 1.0 fusion.131
  117.2 0.1 copy-done.10
  117.3 1.6 fusion.5
  118.9 0.0 copy-done.5
  118.9 2.1 convert_add_fusion
  121.0 2.6 fusion.7
  123.7 7.9 %all-gather.4.cloned.1.call-done = bf16[256,4,2048]{2,1,0:T(4,128)(2,1)} async-done(((bf16[1,4,2048]{2,1,0:T(4,128)(2,1)}), bf16[256,4,2048]{2,1,0:T(4,128)(2,1)}) %all-gather.4.cloned.1.call-update) | async-done | bytes 4194320 | tf_op jit(solution)/shard_map/all_gather | solution.py:21
  131.5 6.9 %reshape.209 = bf16[1024,2048]{1,0:T(8,128)(2,1)} reshape(bf16[256,4,2048]{2,1,0:T(4,128)(2,1)} %all-gather.4.cloned.1.call-done) | data formatting | bytes 8388608
  138.4 2.3 fusion.141
  140.8 0.0 copy-start.12
  140.8 2.4 fusion.140
  143.1 0.0 copy-start.13
  143.2 0.2 exponential_reduce_fusion
  143.4 0.2 exponential_reduce_fusion.1
  143.6 60.9 %all-gather.1 = f32[256,4,2]{1,2,0:T(2,128)S(1)} all-gather(f32[1,4,2]{1,2,0:T(2,128)S(1)} %maximum_bitcast_fusion.1), channel_id=1, replica_groups=mesh['dp_0'=8,'dp_1'=4,'grp_0'=4,'grp_1'=2] {'dp_0','dp_1','grp_0','grp_1'}, dimensions={0}, use_global_device_ids=true | all-gather | bytes 8224 | tf_op jit(solution)/shard_map/all_gather | solution.py:27
  204.5 0.6 subtract_reduce_fusion
  206.5 12.9 %psum.28 = f32[]{:T(128)} all-reduce(f32[]{:T(128)S(6)} %add.150), channel_id=1, replica_groups=mesh['dp_0'=8,'dp_1'=4,'grp_0'=4,'grp_1'=2] {'dp_0'}, use_global_device_ids=true, to_apply=%region_29.30 | all-reduce | flops 1 | bytes 8 | tf_op jit(solution)/shard_map/psum | solution.py:37
  219.3 0.2 reshape.211
  219.5 7.9 %psum.29 = f32[]{:T(128)} all-reduce(f32[]{:T(128)} %psum.28), channel_id=1, replica_groups=mesh['dp_0'=8,'dp_1'=4,'grp_0'=4,'grp_1'=2] {'dp_1'}, use_global_device_ids=true, to_apply=%region_30.31 | all-reduce | flops 1 | bytes 8 | tf_op jit(solution)/shard_map/psum | solution.py:37
  227.4 8.0 %psum.30 = f32[]{:T(128)} all-reduce(f32[]{:T(128)} %psum.29), channel_id=1, replica_groups=mesh['dp_0'=8,'dp_1'=4,'grp_0'=4,'grp_1'=2] {'grp_0'}, use_global_device_ids=true, to_apply=%region_31.32 | all-reduce | flops 1 | bytes 8 | tf_op jit(solution)/shard_map/psum | solution.py:37
  235.4 2.0 fusion.21
  237.4 2.0 fusion.15
  239.4 10.4 %psum.31 = f32[]{:T(128)} all-reduce(f32[]{:T(128)} %psum.30), channel_id=1, replica_groups=mesh['dp_0'=8,'dp_1'=4,'grp_0'=4,'grp_1'=2] {'grp_1'}, use_global_device_ids=true, to_apply=%region_32.33 | all-reduce | flops 1 | bytes 8 | tf_op jit(solution)/shard_map/psum | solution.py:37
  249.8 0.0 copy-done.12
  249.8 2.1 fusion.73
  251.9 0.7 fusion.76
  252.6 2.1 fusion.78
  254.8 0.7 fusion.81
  (38 shorter events, 0.2 us)
Async XLA Ops:
  7.2 5.5 %copy-start = (bf16[4,256,1024]{2,1,0:T(8,128)(2,1)S(1)}, bf16[4,256,1024]{2,1,0:T(8,128)(2,1)}, u32[]{:S(2)}) copy-start(bf16[4,256,1024]{2,1,0:T(8,128)(2,1)} %param.6) | copy-start | bytes 6291460
  7.2 7.8 %copy-start.14 = (s32[4]{0:T(128)S(1)}, s32[4]{0:T(128)}, u32[]{:S(2)}) copy-start(s32[4]{0:T(128)} %param.7) | copy-start | bytes 52
  7.2 124.3 %all-gather.4.cloned.1.call-start = ((), (), s32[]{:S(2)}) async-start(), calls=%async_computation | async-start | bytes 4210688 | tf_op jit(solution)/shard_map/all_gather | solution.py:21
  15.0 1.2 copy-start.6
  15.3 2.9 %copy-start.4 = (bf16[4,256,1024]{2,1,0:T(8,128)(2,1)S(1)}, bf16[4,256,1024]{2,1,0:T(8,128)(2,1)}, u32[]{:S(2)}) copy-start(bf16[4,256,1024]{2,1,0:T(8,128)(2,1)} %param.5) | copy-start | bytes 6291460
  16.3 1.9 copy-start.1
  104.4 4.4 %copy-start.2 = (f32[4,256,1024]{2,1,0:T(8,128)S(1)}, f32[4,256,1024]{2,1,0:T(8,128)}, u32[]{:S(2)}) copy-start(f32[4,256,1024]{2,1,0:T(8,128)} %copy-done.1) | copy-start | bytes 12582916
  104.4 4.6 %copy-start.7 = (f32[4,256,256]{1,2,0:T(8,128)S(1)}, f32[4,256,256]{1,2,0:T(8,128)}, u32[]{:S(2)}) copy-start(f32[4,256,256]{1,2,0:T(8,128)} %copy-done.6) | copy-start | bytes 3145732
  108.7 2.5 copy-start.9
  111.8 4.3 %copy-start.8 = (f32[4,256,256]{1,2,0:T(8,128)S(1)}, f32[4,256,256]{1,2,0:T(8,128)}, u32[]{:S(2)}) copy-start(f32[4,256,256]{1,2,0:T(8,128)} %copy-done.6) | copy-start | bytes 3145732
  111.8 4.3 %copy-start.11 = (bf16[4,256,256]{1,2,0:T(8,128)(2,1)S(1)}, bf16[4,256,256]{1,2,0:T(8,128)(2,1)}, u32[]{:S(2)}) copy-start(bf16[4,256,256]{1,2,0:T(8,128)(2,1)} %get-tuple-element.52) | copy-start | bytes 1572868
  111.8 5.3 %copy-start.3 = (f32[4,256,1024]{2,1,0:T(8,128)S(1)}, f32[4,256,1024]{2,1,0:T(8,128)}, u32[]{:S(2)}) copy-start(f32[4,256,1024]{2,1,0:T(8,128)} %copy-done.1) | copy-start | bytes 12582916
  111.8 5.5 %copy-start.10 = (bf16[4,256,1024]{2,1,0:T(8,128)(2,1)S(1)}, bf16[4,256,1024]{2,1,0:T(8,128)(2,1)}, u32[]{:S(2)}) copy-start(bf16[4,256,1024]{2,1,0:T(8,128)(2,1)} %copy-done.9) | copy-start | bytes 6291460
  117.3 1.6 copy-start.5
  140.8 109.0 %copy-start.12 = (bf16[4,1024]{1,0:T(4,128)(2,1)S(1)}, bf16[4,1024]{1,0:T(4,128)(2,1)}, u32[]{:S(2)}) copy-start(bf16[4,1024]{1,0:T(4,128)(2,1)} %param.8) | copy-start | bytes 24580
  143.1 109.5 %copy-start.13 = (bf16[4,1024]{1,0:T(4,128)(2,1)S(1)}, bf16[4,1024]{1,0:T(4,128)(2,1)}, u32[]{:S(2)}) copy-start(bf16[4,1024]{1,0:T(4,128)(2,1)} %param.9) | copy-start | bytes 24580
Sparse Core Ops, SparseCore 0:
  11.6 119.8 all-gather.3
where the time goes:
time: 266 us; the launch traced here: 264 us
  blocking collectives  100 us (38%)
  local copies, waits for them, and re-layouts  64.9 us (24%)
  other arithmetic  38.3 us (14%)
  matrix products  35.4 us (13%)
  between operations  17.4 us (7%)
  waiting for transfers between devices  7.87 us (3%)
    all_gather x1, blocking collectives, gather_turned(): lax.all_gather(both, axis, axis=0, tiled=True)  60.9 us
    psum x4, blocking collectives, over_axes(): array = lax.psum(array, axis)  39.1 us
    scatter-add x1, other arithmetic, pair_terms(): jnp.diagonal(logits)  26.1 us
    scatter-add x1, local copies, waits for them, and re-layouts, pair_terms(): jnp.diagonal(logits)  19.1 us
    select_n x1, local copies, waits for them, and re-layouts, pair_terms(): masked = jnp.where(both_valid, logits, MASK_FILL)  17.4 us
    mul x1, local copies, waits for them, and re-layouts, pair_terms(): FINE_SCALE * jnp.dot(group_unit.astype(jnp.bfloat16), token_unit.astype(j...  16.5 us
    dot_general x3, matrix products, pair_terms(): jnp.dot(group_unit.astype(jnp.bfloat16), token_unit.astype(jnp.bfloat16)....  10.6 us
    unnamed x33, local copies, waits for them, and re-layouts  9.52 us
  transfers between devices with their start and end apart: 1, of which 1 were waited for; matrix products, arithmetic and copies ran while one was open for 42% of the time, Pallas kernels for 0%

commit v1 on v0

--- a/solution.py
+++ b/solution.py
@@ -12,6 +12,13 @@
 MASK_FILL = -1000000000.0
 
 
+def exchange_gather(x, axis, dim):
+    n_dev = lax.axis_size(axis)
+    pieces = jnp.stack([x for _ in range(n_dev)])
+    pieces = lax.all_to_all(pieces, axis, split_axis=0, concat_axis=0)
+    return jnp.concatenate(pieces, axis=dim)
+
+
 def side_by_side(arrays, axis, dim, along):
     ends, at = ([], 0)
     for a in arrays[:-1]:
@@ -24,7 +31,7 @@
 def gather_turned(arrays, axis, dims):
     turned = [jnp.moveaxis(a, dim, 0) for a, dim in zip(arrays, dims)]
     both = jnp.concatenate([t.reshape(len(t), -1) for t in turned], axis=1)
-    filled, at, gathered = (lax.all_gather(both, axis, axis=0, tiled=True), 0, [])
+    filled, at, gathered = (exchange_gather(both, axis, 0), 0, [])
     for t, dim in zip(turned, dims):
         section = filled[:, at : at + t[0].size].reshape(-1, *t.shape[1:])
         gathered.append(jnp.moveaxis(section, 0, dim))

time: 266 us -> 213 us (0.80)
  blocking collectives: 100 us -> 36 us
  starting transfers between devices: 0.04 us -> 13.4 us
  matrix products: 35.4 us -> 32.4 us
    all_gather x1 -> x0, blocking collectives: 60.9 us -> none  [gather_turned(): lax.all_gather(both, axis, axis=0, tiled=True)]
    all_to_all x0 -> x1, starting transfers between devices: none -> 13.3 us  [exchange_gather(): pieces = lax.all_to_all(pieces, axis, split_axis=0, concat_axis=0)]
    psum x4, blocking collectives: 39.1 us -> 36 us  [over_axes(): array = lax.psum(array, axis)]
    unnamed x33 -> x34, local copies, waits for them, and re-layouts: 9.52 us -> 9.37 us
  transfers between devices with their start and end apart: 1 -> 2, of which waited for: 1 -> 2; matrix products, arithmetic and copies ran while one was open for 42% -> 52% of each run, Pallas kernels for 0% -> 0%
where the time goes in v1:
time: 213 us; the launch traced here: 211 us
  local copies, waits for them, and re-layouts  65.7 us (31%)
  other arithmetic  38.3 us (18%)
  blocking collectives  36 us (17%)
  matrix products  32.4 us (15%)
  between operations  17.4 us (8%)
  starting transfers between devices  13.4 us (6%)
  waiting for transfers between devices  8.13 us (4%)
    psum x4, blocking collectives, over_axes(): array = lax.psum(array, axis)  36 us
    scatter-add x1, other arithmetic, pair_terms(): jnp.diagonal(logits)  26.1 us
    scatter-add x1, local copies, waits for them, and re-layouts, pair_terms(): jnp.diagonal(logits)  19.1 us
    select_n x1, local copies, waits for them, and re-layouts, pair_terms(): masked = jnp.where(both_valid, logits, MASK_FILL)  17.4 us
    mul x1, local copies, waits for them, and re-layouts, pair_terms(): FINE_SCALE * jnp.dot(group_unit.astype(jnp.bfloat16), token_unit.astype(j...  16.5 us
    all_to_all x1, starting transfers between devices, exchange_gather(): pieces = lax.all_to_all(pieces, axis, split_axis=0, concat_axis=0)  13.3 us
    dot_general x3, matrix products, pair_terms(): jnp.dot(group_unit.astype(jnp.bfloat16), token_unit.astype(jnp.bfloat16)....  10.6 us
    unnamed x34, local copies, waits for them, and re-layouts  9.37 us
  transfers between devices with their start and end apart: 2, of which 2 were waited for; matrix products, arithmetic and copies ran while one was open for 52% of the time, Pallas kernels for 0%

profile of v1, /device:TPU:1, one launch (start us, length us, event | category | flops | bytes accessed | tf_op | source)
XLA Modules:
  0.0 211.4 jit_solution(7068607797184535583)
XLA Ops:
  7.2 0.0 copy-start
  7.2 0.0 all-gather.3.cloned.1.call-start
  7.2 1.0 fusion.82
  8.2 0.8 fusion.77
  9.0 0.9 multiply_reduce_fusion.2
  9.9 0.6 maximum_bitcast_fusion
  10.5 0.0 all-gather.3.cloned.1.call-update
  10.6 0.0 copy-start.15
  10.6 2.1 fusion.2
  12.7 2.4 %fusion.133 = (f32[4,256]{1,0:T(4,128)S(1)}, f32[4,256]{1,0:T(4,128)S(1)}, f32[4,256,256]{1,2,0:T(8,128)S(1)}) fusion(bf16[4,256,1024]{2,1,0:T(8,128)(2,1)} %param.5, bf16[4,256,1024]{2,1,0:T(8,128)(2,1)S(1)} %copy-done), kind=kOutput, calls=%fused_computation.192 | convolution fusion | flops 537393152 | bytes 5251072 | tf_op jit(solution)/shard_map/vmap(jvp())/dot_general | solution.py:51
  15.0 0.0 copy-start.7
  15.0 0.2 maximum_reduce_fusion
  15.2 0.1 iota_compare_fusion.1
  15.3 0.9 multiply_reduce_fusion
  16.3 1.9 copy-done.2
  18.2 2.0 fusion.58
  20.2 16.5 %copy.84 = f32[4,256,256]{0,2,1:T(8,128)} copy(f32[4,256,256]{1,2,0:T(8,128)S(1)} %get-tuple-element.46) | data formatting | bytes 2097152 | tf_op jit(solution)/shard_map/vmap(jvp())/mul | solution.py:63
  36.7 2.3 %gather_fusion = f32[256,4]{1,0:T(8,128)S(1)} fusion(f32[4,256,256]{0,2,1:T(8,128)} %copy.84, s32[256]{0:T(256)S(1)} %bitcast.33), kind=kCustom, calls=%fused_computation | custom fusion | bytes 10240 | tf_op jit(solution)/shard_map/vmap(jvp(jit(diagonal)))/cond/branch_0_fun/gather | solution.py:74
  39.0 0.1 copy.90
  39.1 0.5 fusion.55
  39.7 0.3 fusion.56
  40.0 0.2 fusion.110
  40.2 1.4 and_select_fusion
  41.6 17.4 %copy.78 = f32[4,256,256]{0,2,1:T(8,128)} copy(f32[4,256,256]{1,2,0:T(8,128)} %and_select_fusion) | data formatting | bytes 2097152 | tf_op jit(solution)/shard_map/vmap(transpose(jvp(jit(_where))))/select_n | solution.py:71
  59.0 0.1 copy.79
  59.2 26.1 %scatter_fusion = f32[4,256,256]{0,2,1:T(8,128)} fusion(f32[4,256,256]{0,2,1:T(8,128)} %copy.78, s32[256]{0:T(256)S(1)} %bitcast.32, f32[256,4]{1,0:T(8,128)S(1)} %copy.79), kind=kCustom, calls=%fused_computation.1 | custom fusion | flops 1024 | bytes 14336 | tf_op jit(solution)/shard_map/vmap(transpose(jvp(jit(diagonal))))/cond/branch_0_fun/scatter-add | solution.py:74
  85.2 19.1 %copy.80 = f32[4,256,256]{1,2,0:T(8,128)S(1)} copy(f32[4,256,256]{0,2,1:T(8,128)} %scatter_fusion) | data formatting | bytes 2097152 | tf_op jit(solution)/shard_map/vmap(transpose(jvp(jit(diagonal))))/cond/branch_0_fun/scatter-add | solution.py:74
  104.3 0.0 copy-start.8
  104.3 4.3 %fusion = (f32[4,256]{1,0:T(4,128)S(1)}, bf16[4,256,1024]{2,1,0:T(8,128)(2,1)S(1)}) fusion(f32[4,256,1024]{2,1,0:T(8,128)} %copy-done.2, bf16[4,256,1024]{2,1,0:T(8,128)(2,1)} %param.5, f32[4,256]{1,0:T(4,128)S(1)} %get-tuple-element.61, f32[4,256,256]{1,2,0:T(8,128)S(1)} %copy.80), kind=kOutput, calls=%fused_computation.11 | convolution fusion | flops 544472064 | bytes 9445376 | tf_op jit(solution)/shard_map/vmap(transpose(jvp()))/dot_general | solution.py:63
  108.6 0.0 copy-start.10
  108.7 0.3 copy-done.8
  108.9 2.2 %fusion.52 = (f32[4,256]{1,0:T(4,128)S(1)}, bf16[4,256,256]{1,2,0:T(8,128)(2,1)}) fusion(f32[4,256]{1,0:T(4,128)S(1)} %multiply_divide_fusion.1, f32[4,256]{1,0:T(4,128)S(1)} %get-tuple-element.27, f32[4,256,256]{1,2,0:T(8,128)S(1)} %copy-done.8, f32[4,256]{1,0:T(4,128)S(1)} %get-tuple-element.15, bf16[4,256,1024]{2,1,0:T(8,128)(2,1)S(1)} %copy-done, ...), kind=kOutput, calls=%fused_computation.56 | convolution fusion | flops 544472064 | bytes 9986048 | tf_op jit(solution)/shard_map/vmap(transpose(jvp()))/dot_general | solution.py:57
  111.2 0.6 divide_reduce_fusion
  111.8 4.3 %fusion.4 = (f32[4,256]{1,0:T(4,128)S(1)}, bf16[4,256,1024]{2,1,0:T(8,128)(2,1)S(1)}) fusion(bf16[4,256,1024]{2,1,0:T(8,128)(2,1)} %param.5, f32[4,256,1024]{2,1,0:T(8,128)} %copy-done.2, f32[4,256]{1,0:T(4,128)S(1)} %get-tuple-element.62, f32[4,256,256]{1,2,0:T(8,128)S(1)} %copy.80), kind=kOutput, calls=%fused_computation.15 | convolution fusion | flops 544472064 | bytes 9445376 | tf_op jit(solution)/shard_map/vmap(transpose(jvp()))/dot_general | solution.py:63
  116.1 0.0 copy-done.9
  116.1 0.0 copy-done.12
  116.1 1.0 fusion.131
  117.1 0.1 copy-done.11
  117.3 1.6 fusion.5
  118.9 2.1 %convert_add_fusion = bf16[4,256,1024]{2,1,0:T(8,128)(2,1)} fusion(bf16[4,256,1024]{2,1,0:T(8,128)(2,1)S(1)} %fusion.5, bf16[4,256,1024]{2,1,0:T(8,128)(2,1)S(1)} %copy-done.6, pred[4,256,256]{1,2,0:T(32,128)(4,1)S(1)} %get-tuple-element.31, pred[4,256,256]{1,2,0:T(32,128)(4,1)S(1)} %get-tuple-element.33, f32[4,256]{1,0:T(4,128)S(1)} %get-tuple-element.40, ...), kind=kOutput, calls=%fused_computation.21 | convolution fusion | flops 540278784 | bytes 7876608 | tf_op jit(solution)/shard_map/vmap(transpose(jvp()))/dot_general | solution.py:51
  121.0 2.6 %fusion.7 = bf16[4,256,1024]{2,1,0:T(8,128)(2,1)} fusion(bf16[4,256,1024]{2,1,0:T(8,128)(2,1)S(1)} %copy-done.6, bf16[4,256,1024]{2,1,0:T(8,128)(2,1)S(1)} %get-tuple-element.48, f32[4,256]{1,0:T(4,128)S(1)} %multiply_multiply_fusion.1, f32[4,256]{1,0:T(4,128)S(1)} %get-tuple-element.61, bf16[4,256,1024]{2,1,0:T(8,128)(2,1)S(1)} %copy-done, ...), kind=kOutput, calls=%fused_computation.20 | convolution fusion | flops 547618816 | bytes 9981952 | tf_op jit(solution)/shard_map/vmap(transpose(jvp()))/dot_general | solution.py:51
  123.6 7.9 %all-gather.3.cloned.1.call-done = bf16[256,4,2048]{2,1,0:T(4,128)(2,1)} async-done(((bf16[1,4,2048]{2,1,0:T(4,128)(2,1)}), bf16[256,4,2048]{2,1,0:T(4,128)(2,1)}) %all-gather.3.cloned.1.call-update) | async-done | bytes 4194320 | tf_op jit(solution)/shard_map/all_gather | solution.py:28
  131.5 6.9 %reshape.215 = bf16[1024,2048]{1,0:T(8,128)(2,1)} reshape(bf16[256,4,2048]{2,1,0:T(4,128)(2,1)} %all-gather.3.cloned.1.call-done) | data formatting | bytes 8388608
  138.4 2.3 %fusion.141 = (f32[4]{0:T(128)S(1)}, f32[4,1024]{1,0:T(4,128)S(1)}) fusion(bf16[4,1024]{1,0:T(4,128)(2,1)S(1)} %get-tuple-element.21, bf16[1024,2048]{1,0:T(8,128)(2,1)} %reshape.215), kind=kOutput, calls=%fused_computation.195 | convolution fusion | flops 8396796 | bytes 2121744 | tf_op jit(solution)/shard_map/dot_general | solution.py:111
  140.8 0.0 copy-start.13
  140.8 2.4 %fusion.140 = (f32[4]{0:T(128)S(1)}, f32[4,1024]{1,0:T(4,128)S(1)}) fusion(bf16[4,1024]{1,0:T(4,128)(2,1)S(1)} %get-tuple-element.22, bf16[1024,2048]{1,0:T(8,128)(2,1)} %reshape.215), kind=kOutput, calls=%fused_computation.194 | convolution fusion | flops 8396796 | bytes 2121744 | tf_op jit(solution)/shard_map/dot_general | solution.py:112
  143.1 0.0 copy-start.14
  143.2 0.2 exponential_reduce_fusion
  143.4 0.2 exponential_reduce_fusion.1
  143.6 0.6 subtract_reduce_fusion
  145.5 13.0 %psum.28 = f32[]{:T(128)} all-reduce(f32[]{:T(128)S(6)} %add.150), channel_id=1, replica_groups=mesh['dp_0'=8,'dp_1'=4,'grp_0'=4,'grp_1'=2] {'dp_0'}, use_global_device_ids=true, to_apply=%region_29.30 | all-reduce | flops 1 | bytes 8 | tf_op jit(solution)/shard_map/psum | solution.py:44
  158.5 8.7 %psum.29 = f32[]{:T(128)} all-reduce(f32[]{:T(128)} %psum.28), channel_id=1, replica_groups=mesh['dp_0'=8,'dp_1'=4,'grp_0'=4,'grp_1'=2] {'dp_1'}, use_global_device_ids=true, to_apply=%region_30.31 | all-reduce | flops 1 | bytes 8 | tf_op jit(solution)/shard_map/psum | solution.py:44
  167.2 0.8 stack.2
  167.9 13.3 %all-to-all-start = ((f32[256,4,2]{1,2,0:T(2,128)}), f32[256,4,2]{1,2,0:T(2,128)S(1)}, u32[]{:S(2)}, u32[]{:S(2)}) async-start(f32[256,4,2]{1,2,0:T(2,128)} %stack.2), calls=%async_computation | async-start | bytes 524288 | tf_op jit(solution)/shard_map/all_to_all | solution.py:18
  181.2 9.8 %psum.30 = f32[]{:T(128)} all-reduce(f32[]{:T(128)} %psum.29), channel_id=1, replica_groups=mesh['dp_0'=8,'dp_1'=4,'grp_0'=4,'grp_1'=2] {'grp_0'}, use_global_device_ids=true, to_apply=%region_31.32 | all-reduce | flops 1 | bytes 8 | tf_op jit(solution)/shard_map/psum | solution.py:44
  191.0 4.6 %psum.31 = f32[]{:T(128)} all-reduce(f32[]{:T(128)} %psum.30), channel_id=1, replica_groups=mesh['dp_0'=8,'dp_1'=4,'grp_0'=4,'grp_1'=2] {'grp_1'}, use_global_device_ids=true, to_apply=%region_32.33 | all-reduce | flops 1 | bytes 8 | tf_op jit(solution)/shard_map/psum | solution.py:44
  196.3 0.3 all-to-all-done
  196.5 0.2 reshape.201
  196.7 2.2 %fusion.21 = f32[4,1024]{1,0:T(4,128)S(1)} fusion(bf16[1024,2048]{1,0:T(8,128)(2,1)} %reshape.215, f32[4,1024]{1,0:T(4,128)S(1)} %get-tuple-element.56, f32[1024]{0:T(1024)S(1)} %bitcast.35, s32[4]{0:T(128)S(1)} %iota_add_fusion), kind=kOutput, calls=%fused_computation.35 | convolution fusion | flops 8413184 | bytes 2134032 | tf_op jit(solution)/shard_map/dot_general | solution.py:127
  198.9 2.0 fusion.15
  200.9 0.5 fusion.73
  201.5 0.7 fusion.76
  202.2 0.5 fusion.78
  202.7 0.7 fusion.81
  (42 shorter events, 0.2 us)
Async XLA Ops:
  7.2 5.5 %copy-start = (bf16[4,256,1024]{2,1,0:T(8,128)(2,1)S(1)}, bf16[4,256,1024]{2,1,0:T(8,128)(2,1)}, u32[]{:S(2)}) copy-start(bf16[4,256,1024]{2,1,0:T(8,128)(2,1)} %param.6) | copy-start | bytes 6291460
  7.2 124.3 %all-gather.3.cloned.1.call-start = ((), (), s32[]{:S(2)}) async-start(), calls=%async_computation.1 | async-start | bytes 4210688 | tf_op jit(solution)/shard_map/all_gather | solution.py:28
  10.6 4.7 %copy-start.15 = (s32[4]{0:T(128)S(1)}, s32[4]{0:T(128)}, u32[]{:S(2)}) copy-start(s32[4]{0:T(128)} %param.7) | copy-start | bytes 52
  15.0 1.2 copy-start.7
  15.3 2.9 %copy-start.5 = (bf16[4,256,1024]{2,1,0:T(8,128)(2,1)S(1)}, bf16[4,256,1024]{2,1,0:T(8,128)(2,1)}, u32[]{:S(2)}) copy-start(bf16[4,256,1024]{2,1,0:T(8,128)(2,1)} %param.5) | copy-start | bytes 6291460
  16.2 1.9 copy-start.2
  104.3 4.3 %copy-start.3 = (f32[4,256,1024]{2,1,0:T(8,128)S(1)}, f32[4,256,1024]{2,1,0:T(8,128)}, u32[]{:S(2)}) copy-start(f32[4,256,1024]{2,1,0:T(8,128)} %copy-done.2) | copy-start | bytes 12582916
  104.3 4.6 %copy-start.8 = (f32[4,256,256]{1,2,0:T(8,128)S(1)}, f32[4,256,256]{1,2,0:T(8,128)}, u32[]{:S(2)}) copy-start(f32[4,256,256]{1,2,0:T(8,128)} %copy-done.7) | copy-start | bytes 3145732
  108.6 2.5 %copy-start.10 = (bf16[4,256,1024]{2,1,0:T(8,128)(2,1)}, bf16[4,256,1024]{2,1,0:T(8,128)(2,1)S(1)}, u32[]{:S(2)}) copy-start(bf16[4,256,1024]{2,1,0:T(8,128)(2,1)S(1)} %get-tuple-element.50) | copy-start | bytes 6291460
  111.8 4.3 %copy-start.9 = (f32[4,256,256]{1,2,0:T(8,128)S(1)}, f32[4,256,256]{1,2,0:T(8,128)}, u32[]{:S(2)}) copy-start(f32[4,256,256]{1,2,0:T(8,128)} %copy-done.7) | copy-start | bytes 3145732
  111.8 4.3 %copy-start.12 = (bf16[4,256,256]{1,2,0:T(8,128)(2,1)S(1)}, bf16[4,256,256]{1,2,0:T(8,128)(2,1)}, u32[]{:S(2)}) copy-start(bf16[4,256,256]{1,2,0:T(8,128)(2,1)} %get-tuple-element.52) | copy-start | bytes 1572868
  111.8 5.4 %copy-start.4 = (f32[4,256,1024]{2,1,0:T(8,128)S(1)}, f32[4,256,1024]{2,1,0:T(8,128)}, u32[]{:S(2)}) copy-start(f32[4,256,1024]{2,1,0:T(8,128)} %copy-done.2) | copy-start | bytes 12582916
  111.8 5.5 %copy-start.11 = (bf16[4,256,1024]{2,1,0:T(8,128)(2,1)S(1)}, bf16[4,256,1024]{2,1,0:T(8,128)(2,1)}, u32[]{:S(2)}) copy-start(bf16[4,256,1024]{2,1,0:T(8,128)(2,1)} %copy-done.10) | copy-start | bytes 6291460
  117.3 1.6 copy-start.6
  140.8 60.2 %copy-start.13 = (bf16[4,1024]{1,0:T(4,128)(2,1)S(1)}, bf16[4,1024]{1,0:T(4,128)(2,1)}, u32[]{:S(2)}) copy-start(bf16[4,1024]{1,0:T(4,128)(2,1)} %param.8) | copy-start | bytes 24580
  143.1 59.0 %copy-start.14 = (bf16[4,1024]{1,0:T(4,128)(2,1)S(1)}, bf16[4,1024]{1,0:T(4,128)(2,1)}, u32[]{:S(2)}) copy-start(bf16[4,1024]{1,0:T(4,128)(2,1)} %param.9) | copy-start | bytes 24580
  167.9 28.6 %all-to-all-start = ((f32[256,4,2]{1,2,0:T(2,128)}), f32[256,4,2]{1,2,0:T(2,128)S(1)}, u32[]{:S(2)}, u32[]{:S(2)}) async-start(f32[256,4,2]{1,2,0:T(2,128)} %stack.2), calls=%async_computation | async-start | bytes 524288 | tf_op jit(solution)/shard_map/all_to_all | solution.py:18
  196.7 4.2 %copy-start.1 = (bf16[1024,2048]{1,0:T(8,128)(2,1)S(1)}, bf16[1024,2048]{1,0:T(8,128)(2,1)}, u32[]{:S(2)}) copy-start(bf16[1024,2048]{1,0:T(8,128)(2,1)} %reshape.215) | copy-start | bytes 12582916
Sparse Core Ops, SparseCore 0:
  11.6 119.8 all-gather.2
